TPU v7x, 32 devices: a whole 2x2x4 slice. The times are simulated.
32 devices in a mesh: freq: 4 (over y, x), clus: 8 (over z, core).
Axes of the slice: x: 2, y: 2, z: 4, core: 2. Of those that a mesh axis runs over, the one named last changes fastest.
Arguments:
- history: bfloat16 [1024, 8, 1024], P('freq', None, 'clus'), may hold values from -6 to 6
- near_blocks: bfloat16 [8, 4, 512, 2, 128, 128], P('clus', None, 'freq'), may hold values from -0.1875 to 0.1875
- near_list: int32 [8, 4], replicated, may hold values from 0 to 7, as said below
- basis_out: bfloat16 [512, 2, 32, 1024], P('freq', None, None, 'clus'), may hold values from -0.75 to 0.75
- basis_in: bfloat16 [512, 2, 32, 1024], P('freq', None, None, 'clus'), may hold values from -0.375 to 0.375
- coupling: bfloat16 [8, 512, 2, 32, 256], P('clus', 'freq'), may hold values from -0.375 to 0.375
- ranks: int32 [8, 512, 8], P('clus', 'freq'), may hold values from 4 to 32
Outputs:
- potential: bfloat16 [512, 2, 8, 1024], P('freq', None, None, 'clus')
Inputs may be any that keep to these rules, and one draw needn't show every extreme that they name: `near_list`: row t starts with t itself; its other 3 entries are distinct shards other than t, each (t + d) mod 8 for some d with 1 <= |d| <= 3.
All inputs are finite; a program needn't handle non-finite values.
Results may differ from a plain program's by a relative error of at most 0.0055.
Values may be sent and summed in bfloat16 or wider, within the bound.
A program may use at most 128 MiB of HBM per device.

v0:
```python
import functools
import math

import jax
import jax.numpy as jnp
from jax import lax
from jax.experimental import pallas as pl
from jax.experimental.pallas import tpu as pltpu
from jax.sharding import PartitionSpec as P

LANES = 128
NT = (((1,), (1,)), ((), ()))
NN = (((1,), (0,)), ((), ()))


def dot(left, right, dims):
    return lax.dot_general(left, right, dims, preferred_element_type=jnp.float32)


def wave_factors(first_wave, count, total):
    waves = (first_wave + lax.iota(jnp.int32, count))[:, None]

    def factor(steps, scale):
        angle = (waves * steps[None, :] % total).astype(jnp.float32) * (2.0 * math.pi / total)
        weight = jnp.exp(steps.astype(jnp.float32) * (-math.log(2.0) / total)) * scale
        return weight[None, :] * jnp.cos(angle), -weight[None, :] * jnp.sin(angle)

    coarse = factor(lax.iota(jnp.int32, total // LANES) * LANES, 1.0)
    fine = factor(lax.iota(jnp.int32, LANES), total ** (-0.5))
    return coarse + fine


def fill_tables(coarse_re, coarse_im, fine_re, fine_im, high, low):
    count = fine_re.shape[0]
    for a in range(coarse_re.shape[1]):
        c_re, c_im = coarse_re[:, a : a + 1], coarse_im[:, a : a + 1]
        f_re, f_im = fine_re[...], fine_im[...]
        for part, value in ((0, c_re * f_re - c_im * f_im), (1, c_re * f_im + c_im * f_re)):
            top = value.astype(jnp.bfloat16)
            rows, cols = pl.ds(part * count, count), pl.ds(a * LANES, LANES)
            high[rows, cols] = top
            low[rows, cols] = (value - top.astype(jnp.float32)).astype(jnp.bfloat16)


def transform_one(e, hist, high, low, sums):
    blocks, length = hist.shape[0], hist.shape[2]
    waves = high.shape[0] // 2
    exc = hist.shape[1]
    steps = jnp.concatenate([hist[f, e] for f in range(blocks)], axis=0)
    value = dot(high[...], steps, NN) + dot(low[...], steps, NN)
    for part in range(2):
        sums[pl.ds(part * exc + e, waves, stride=2 * exc), :] = value[part * waves : (part + 1) * waves]


def compress(group, pack, dens, basis_in, coeffs):
    rows, rank = dens.shape[1], basis_in.shape[2]
    half = rows // 2
    waves = pl.ds(group * pack, pack)
    left = dens[waves].reshape(pack * rows, LANES)
    lane = lax.broadcasted_iota(jnp.int32, (rows, LANES), 1) // rank

    def pick(part):
        full = dot(left, basis_in[waves, part].reshape(pack * rank, LANES), NT)
        out = full[:rows]
        for w in range(1, pack):
            out = jnp.where(lane == w, full[w * rows : (w + 1) * rows], out)
        return out

    by_re, by_im = pick(0), pick(1)
    real = by_re[:half] - by_im[half:]
    imag = by_re[half:] + by_im[:half]
    coeffs[group] = jnp.concatenate([real, imag], 0).astype(jnp.bfloat16)


def transform_kernel(c_re, c_im, f_re, f_im, hist, basis_in, dens, coeffs, high, low, sums):
    fill_tables(c_re, c_im, f_re, f_im, high, low)
    for e in range(hist.shape[1]):
        transform_one(e, hist, high, low, sums)
    dens[...] = sums[...].reshape(dens.shape).astype(jnp.bfloat16)
    pack = LANES // basis_in.shape[2]

    def step(group, carry):
        compress(group, pack, dens, basis_in, coeffs)
        return carry

    lax.fori_loop(0, coeffs.shape[0], step, 0)


def apply_kernel(mine, near, dens, coeffs, couple, basis_out, limit, out):
    slots, waves = near.shape[1], near.shape[2]
    panels, rank = near.shape[4], couple.shape[3]
    sources, rows = dens.shape[0], dens.shape[2]
    half = rows // 2
    pack = LANES // rank
    picked = [mine[j] for j in range(slots)]
    position = lax.broadcasted_iota(jnp.int32, (rank, sources * rank), 0)

    def step(group, carry):
        packed = [coeffs[s, group].astype(jnp.float32) for s in range(sources)]
        for w in range(pack):
            k = group * pack + w
            left = jnp.concatenate([dens[s, k] for s in picked], axis=1)
            right = jnp.concatenate(
                [near[0, j, k].reshape(2 * panels, panels) for j in range(slots)], axis=1
            )
            both = dot(left, right, NT)
            stacked = jnp.concatenate(
                [p[:, w * rank : (w + 1) * rank] for p in packed], axis=1
            ).astype(jnp.bfloat16)
            keep = position < limit[pl.ds(k, 1), :]

            def mix(part):
                value = couple[0, k, part]
                return dot(stacked, jnp.where(keep, value, jnp.zeros_like(value)), NT)

            by_re, by_im = mix(0), mix(1)
            mixed = jnp.concatenate(
                [by_re[:half] - by_im[half:], by_re[half:] + by_im[:half]], 0
            ).astype(jnp.bfloat16)
            spread = jnp.concatenate([basis_out[k, 0], basis_out[k, 1]], axis=1)
            both = both + dot(mixed, spread, NN)
            by_re, by_im = both[:, :panels], both[:, panels:]
            out[k, 0] = (by_re[:half] - by_im[half:]).astype(out.dtype)
            out[k, 1] = (by_re[half:] + by_im[:half]).astype(out.dtype)
        return carry

    lax.fori_loop(0, waves // pack, step, 0)


def apply_all(mine, near_blocks, dens, coeffs, coupling, basis_out, limit):
    waves, panels = basis_out.shape[0], basis_out.shape[3]
    rank, slots = basis_out.shape[2], near_blocks.shape[1]
    sources, _, rows, _ = dens.shape
    step = min(waves, 8)
    pack = LANES // rank
    grid_spec = pltpu.PrefetchScalarGridSpec(
        num_scalar_prefetch=1,
        grid=(waves // step,),
        in_specs=[
            pl.BlockSpec((1, slots, step, 2, panels, panels), lambda g, m: (0, 0, g, 0, 0, 0)),
            pl.BlockSpec((sources, step, rows, panels), lambda g, m: (0, g, 0, 0)),
            pl.BlockSpec((sources, step // pack, rows, LANES), lambda g, m: (0, g, 0, 0)),
            pl.BlockSpec((1, step, 2, rank, sources * rank), lambda g, m: (0, g, 0, 0, 0)),
            pl.BlockSpec((step, 2, rank, panels), lambda g, m: (g, 0, 0, 0)),
            pl.BlockSpec((step, sources * rank), lambda g, m: (g, 0)),
        ],
        out_specs=pl.BlockSpec((step, 2, rows // 2, panels), lambda g, m: (g, 0, 0, 0)),
    )
    return pl.pallas_call(
        apply_kernel,
        out_shape=jax.ShapeDtypeStruct((waves, 2, rows // 2, panels), jnp.bfloat16),
        grid_spec=grid_spec,
    )(mine, near_blocks, dens, coeffs, coupling, basis_out, limit)


def local(history, near_blocks, near_list, basis_out, basis_in, coupling, ranks):
    steps_dev, exc, panels = history.shape
    waves_dev, _, rank, _ = basis_in.shape
    clusters = lax.axis_size("clus")
    freqs = lax.axis_size("freq")
    total = steps_dev * freqs
    pack = LANES // rank
    mine = lax.dynamic_index_in_dim(near_list, lax.axis_index("clus"), 0, keepdims=False)
    nearby = jnp.any(mine[:, None] == lax.iota(jnp.int32, clusters)[None, :], axis=0)
    far = jnp.where(nearby[None, :], 0, ranks[0])
    within = lax.iota(jnp.int32, rank)
    limit = jnp.where(within[None, None, :] < far[:, :, None], far[:, :, None], 0)
    limit = limit.reshape(waves_dev, clusters * rank)
    factors = wave_factors(lax.axis_index("freq") * waves_dev, waves_dev, total)
    turned = jnp.transpose(history, (1, 0, 2))
    hist = lax.all_gather(turned, "freq", axis=0)
    dens, coeffs = pl.pallas_call(
        transform_kernel,
        out_shape=(
            jax.ShapeDtypeStruct((waves_dev, 2 * exc, panels), jnp.bfloat16),
            jax.ShapeDtypeStruct((waves_dev // pack, 2 * exc, LANES), jnp.bfloat16),
        ),
        scratch_shapes=[
            pltpu.VMEM((2 * waves_dev, total), jnp.bfloat16),
            pltpu.VMEM((2 * waves_dev, total), jnp.bfloat16),
            pltpu.VMEM((waves_dev * 2 * exc, panels), jnp.float32),
        ],
    )(*factors, hist, basis_in)
    dens = lax.all_gather(dens, "clus", axis=0)
    coeffs = lax.all_gather(coeffs, "clus", axis=0)
    return apply_all(mine, near_blocks, dens, coeffs, coupling, basis_out, limit)


def solution(mesh):
    placed = (
        P("freq", None, "clus"),
        P("clus", None, "freq", None, None, None),
        P(),
        P("freq", None, None, "clus"),
        P("freq", None, None, "clus"),
        P("clus", "freq", None, None, None),
        P("clus", "freq", None),
    )
    return jax.shard_map(
        local, mesh=mesh, in_specs=placed, out_specs=P("freq", None, None, "clus"), check_vma=False
    )
```

profile of v0, /device:TPU:0, one launch (start us, length us, event | category | flops | bytes accessed | tf_op | source)
XLA Modules:
  0.0 167.4 jit_solution(9311347818261553846)
XLA Ops:
  6.5 0.0 copy-start
  6.5 0.0 all-gather.7.cloned.1.call-start
  6.5 0.7 all-gather.7.cloned.1.call-update
  7.3 0.0 all-gather.11.cloned.1.call-start
  7.4 1.0 sine_multiply_fusion
  8.4 1.0 sine_multiply_fusion.1
  9.4 37.6 %all-gather.7.cloned.1.call-done = bf16[32,256,128]{2,0,1:T(8,128)(2,1)} async-done(((bf16[8,256,128]{2,0,1:T(8,128)(2,1)}), bf16[32,256,128]{2,0,1:T(8,128)(2,1)}) %all-gather.7.cloned.1.call-update) | async-done | bytes 2097168 | tf_op jit(solution)/shard_map/all_gather | solution.py:171
  47.0 3.7 %copy.26 = bf16[32,256,128]{2,1,0:T(8,128)(2,1)} copy(bf16[32,256,128]{2,0,1:T(8,128)(2,1)} %all-gather.7.cloned.1.call-done) | data formatting | bytes 4194304 | tf_op jit(solution)/shard_map/all_gather | solution.py:171
  50.7 0.0 copy-start.1
  50.7 11.0 %shard_map.73 = (bf16[128,16,128]{2,1,0:T(8,128)(2,1)}, bf16[32,16,128]{2,1,0:T(8,128)(2,1)}) custom-call(f32[128,8]{1,0:T(8,128)} %get-tuple-element.10.c_re, f32[128,8]{1,0:T(8,128)} %get-tuple-element.9.c_im, f32[128,128]{1,0:T(8,128)} %get-tuple-element.12.f_re, f32[128,128]{1,0:T(8,128)} %get-tuple-element.11.f_im, bf16[4,8,256,128]{3,2,1,0:T(8,128)(2,1)} %bitcast.7, ...), custom_call_target="tpu_custom_call" | custom-call | tf_op jit(solution)/shard_map/pallas_call | solution.py:172
  61.7 0.0 all-gather.11.cloned.1.call-update
  61.7 0.0 all-gather.9.cloned.1.call-start
  61.7 0.7 all-gather.9.cloned.1.call-update
  62.4 0.1 lt.40
  62.5 0.0 copy-done.1
  62.5 0.1 copy.27
  62.6 0.0 copy-done
  62.6 0.2 dynamic-slice_reduce_fusion.mine
  62.8 0.0 copy-start.2
  62.8 0.1 fusion.9
  63.0 0.1 copy.29
  63.1 0.7 compare_select_fusion.limit
  63.8 20.3 %all-gather.11.cloned.1.call-done = bf16[256,16,128]{2,1,0:T(8,128)(2,1)} async-done(((bf16[32,16,128]{2,1,0:T(8,128)(2,1)}), bf16[256,16,128]{2,1,0:T(8,128)(2,1)}) %all-gather.11.cloned.1.call-update) | async-done | bytes 1048592 | tf_op jit(solution)/shard_map/all_gather | solution.py:185
  84.1 48.1 %all-gather.9.cloned.1.call-done = bf16[1024,16,128]{2,1,0:T(8,128)(2,1)} async-done(((bf16[128,16,128]{2,1,0:T(8,128)(2,1)}), bf16[1024,16,128]{2,1,0:T(8,128)(2,1)}) %all-gather.9.cloned.1.call-update) | async-done | bytes 4194320 | tf_op jit(solution)/shard_map/all_gather | solution.py:184
  132.2 0.0 copy-done.2
  132.2 28.7 %shard_map.74 = bf16[128,2,8,128]{3,2,1,0:T(8,128)(2,1)} custom-call(s32[4]{0:T(128)} %copy-done.2, bf16[1,4,128,2,128,128]{5,4,3,2,1,0:T(8,128)(2,1)} %near.1, bf16[8,128,16,128]{3,2,1,0:T(8,128)(2,1)} %bitcast.8, bf16[8,32,16,128]{3,2,1,0:T(8,128)(2,1)} %bitcast.9, bf16[1,128,2,32,256]{4,3,2,1,0:T(8,128)(2,1)} %couple.1, ...), custom_call_target="tpu_custom_call" | custom-call | tf_op jit(solution)/shard_map/pallas_call | solution.py:149
  (8 shorter events, 0.1 us)
Async XLA Ops:
  6.5 56.1 %copy-start = (s32[8,4]{0,1:T(4,128)S(1)}, s32[8,4]{0,1:T(4,128)}, u32[]{:S(2)}) copy-start(s32[8,4]{0,1:T(4,128)} %param.9) | copy-start | bytes 388
  6.5 40.4 %all-gather.7.cloned.1.call-start = ((), (), s32[]{:S(2)}) async-start(), calls=%async_computation | async-start | bytes 2621440 | tf_op jit(solution)/shard_map/all_gather | solution.py:171
  7.3 76.8 %all-gather.11.cloned.1.call-start = ((), (), s32[]{:S(2)}) async-start(), calls=%async_computation.2 | async-start | bytes 1179648 | tf_op jit(solution)/shard_map/all_gather | solution.py:185
  50.7 11.8 %copy-start.1 = (s32[1,128,8]{1,2,0:T(8,128)S(1)}, s32[1,128,8]{1,2,0:T(8,128)}, u32[]{:S(2)}) copy-start(s32[1,128,8]{1,2,0:T(8,128)} %param.13) | copy-start | bytes 12292
  61.7 70.5 %all-gather.9.cloned.1.call-start = ((), (), s32[]{:S(2)}) async-start(), calls=%async_computation.1 | async-start | bytes 4718592 | tf_op jit(solution)/shard_map/all_gather | solution.py:184
  62.8 69.4 %copy-start.2 = (s32[4]{0:T(128)}, s32[4]{0:T(128)S(1)}, u32[]{:S(2)}) copy-start(s32[4]{0:T(128)S(1)} %dynamic-slice_reduce_fusion.mine) | copy-start | bytes 52
Sparse Core Ops, SparseCore 0:
  9.2 37.7 all-gather.6
  61.8 22.2 all-gather.10
  85.7 46.4 all-gather.8
where the time goes:
time: 168 us; the launch traced here: 167 us
  waiting for transfers between devices  107 us (64%)
  Pallas kernels  39.6 us (24%)
  between operations  13.2 us (8%)
  local copies, waits for them, and re-layouts  4.29 us (3%)
  other arithmetic  2.79 us (2%)
    all_gather x1, waiting for transfers between devices, local(): dens = lax.all_gather(dens, 'clus', axis=0)  48.1 us
    all_gather x1, waiting for transfers between devices, local(): hist = lax.all_gather(turned, 'freq', axis=0)  37.6 us
    pallas_call x1, Pallas kernels, apply_all(): pl.pallas_call(apply_kernel, out_shape=jax.ShapeDtypeStruct((waves, 2, ro...  28.7 us
    all_gather x1, waiting for transfers between devices, local(): coeffs = lax.all_gather(coeffs, 'clus', axis=0)  20.3 us
    pallas_call x1, Pallas kernels, local(): pl.pallas_call(transform_kernel, out_shape=(jax.ShapeDtypeStruct((waves_d...  11 us
    all_gather x1, local copies, waits for them, and re-layouts, local(): hist = lax.all_gather(turned, 'freq', axis=0)  3.73 us
  transfers between devices with their start and end apart: 3, of which 3 were waited for; matrix products, arithmetic and copies ran while one was open for 2% of the time, Pallas kernels for 0%

commit v1 on v0

v1 whole, which is shorter than its diff:
```python
import functools
import math

import jax
import jax.numpy as jnp
from jax import lax
from jax.experimental import pallas as pl
from jax.experimental.pallas import tpu as pltpu
from jax.sharding import PartitionSpec as P

LANES = 128
NT = (((1,), (1,)), ((), ()))
NN = (((1,), (0,)), ((), ()))


def dot(left, right, dims):
    return lax.dot_general(left, right, dims, preferred_element_type=jnp.float32)


def wave_factors(first_wave, count, total):
    waves = (first_wave + lax.iota(jnp.int32, count))[:, None]

    def factor(steps, scale):
        angle = (waves * steps[None, :] % total).astype(jnp.float32) * (2.0 * math.pi / total)
        weight = jnp.exp(steps.astype(jnp.float32) * (-math.log(2.0) / total)) * scale
        return weight[None, :] * jnp.cos(angle), -weight[None, :] * jnp.sin(angle)

    coarse = factor(lax.iota(jnp.int32, total // LANES) * LANES, 1.0)
    fine = factor(lax.iota(jnp.int32, LANES), total ** (-0.5))
    return coarse + fine


CHUNKS = 4
MESH = pl.DeviceIdType.MESH


def fill_tables(coarse_re, coarse_im, fine_re, fine_im, table):
    waves = fine_re.shape[0]
    chunk = waves // CHUNKS
    for a in range(coarse_re.shape[1]):
        c_re, c_im = coarse_re[:, a : a + 1], coarse_im[:, a : a + 1]
        f_re, f_im = fine_re[...], fine_im[...]
        for part, value in ((0, c_re * f_re - c_im * f_im), (1, c_re * f_im + c_im * f_re)):
            high = value.astype(jnp.bfloat16)
            low = (value - high.astype(jnp.float32)).astype(jnp.bfloat16)
            for w in range(CHUNKS):
                for piece, held in ((0, high), (1, low)):
                    rows = pl.ds((2 * piece + part) * chunk, chunk)
                    table[w, rows, a * LANES : (a + 1) * LANES] = held[w * chunk : (w + 1) * chunk]


def transform_chunk(w, hist, table, sums, buf, me):
    blocks, exc, length = hist.shape[0], hist.shape[1], hist.shape[2]
    half = table.shape[1] // 2
    chunk = half // 2
    for e in range(0, exc, 2):
        value = None
        for f in range(blocks):
            steps = jnp.concatenate([hist[f, e], hist[f, e + 1]], axis=1)
            term = dot(table[w, :, f * length : (f + 1) * length], steps, NN)
            value = term if value is None else value + term
        value = value[:half] + value[half:]
        for part in range(2):
            for side in range(2):
                sums[pl.ds(part * exc + e + side, chunk, stride=2 * exc), :] = value[
                    part * chunk : (part + 1) * chunk, side * LANES : (side + 1) * LANES
                ]
    buf[me, pl.ds(0, chunk)] = sums[...].reshape(chunk, 2 * exc, LANES).astype(jnp.bfloat16)


def compress_chunk(w, buf, basis_in, me, chunk):
    rows, rank = buf.shape[2], basis_in.shape[2]
    half = rows // 2
    pack = LANES // rank
    lane = lax.broadcasted_iota(jnp.int32, (rows, LANES), 1) // rank

    def step(group, carry):
        left = buf[me, pl.ds(group * pack, pack)].reshape(pack * rows, LANES)

        def pick(part):
            right = basis_in[pl.ds(w * chunk + group * pack, pack), part]
            full = dot(left, right.reshape(pack * rank, LANES), NT)
            out = full[:rows]
            for i in range(1, pack):
                out = jnp.where(lane == i, full[i * rows : (i + 1) * rows], out)
            return out

        by_re, by_im = pick(0), pick(1)
        real = by_re[:half] - by_im[half:]
        imag = by_re[half:] + by_im[:half]
        buf[me, chunk + group] = jnp.concatenate([real, imag], 0).astype(jnp.bfloat16)
        return carry

    lax.fori_loop(0, chunk // pack, step, 0)


def apply_chunk(w, picked, near, buf, couple, basis_out, limit, out):
    slots, chunk = near.shape[1], near.shape[2]
    panels, rank = near.shape[4], couple.shape[2]
    sources, rows = buf.shape[0], buf.shape[2]
    half = rows // 2
    pack = LANES // rank
    position = lax.broadcasted_iota(jnp.int32, (rank, sources * rank), 0)

    def step(group, carry):
        packed = [buf[s, chunk + group].astype(jnp.float32) for s in range(sources)]
        for i in range(pack):
            k = group * pack + i
            wave = w * chunk + k
            left = jnp.concatenate([buf[s, k] for s in picked], axis=1)
            right = jnp.concatenate(
                [near[w, j, k].reshape(2 * panels, panels) for j in range(slots)], axis=1
            )
            both = dot(left, right, NT)
            stacked = jnp.concatenate(
                [p[:, i * rank : (i + 1) * rank] for p in packed], axis=1
            ).astype(jnp.bfloat16)
            keep = position < limit[pl.ds(wave, 1), :]

            def mix(part):
                value = couple[wave, part]
                return dot(stacked, jnp.where(keep, value, jnp.zeros_like(value)), NT)

            by_re, by_im = mix(0), mix(1)
            mixed = jnp.concatenate(
                [by_re[:half] - by_im[half:], by_re[half:] + by_im[:half]], 0
            ).astype(jnp.bfloat16)
            spread = jnp.concatenate([basis_out[wave, 0], basis_out[wave, 1]], axis=1)
            both = both + dot(mixed, spread, NN)
            by_re, by_im = both[:, :panels], both[:, panels:]
            out[wave, 0] = (by_re[:half] - by_im[half:]).astype(out.dtype)
            out[wave, 1] = (by_re[half:] + by_im[:half]).astype(out.dtype)
        return carry

    lax.fori_loop(0, chunk // pack, step, 0)


def kernel(freqs, clusters, mine, c_re, c_im, f_re, f_im, limit, own, near_in, couple_in, out_in, in_in,
           out, hist, table, sums, near, couple, basis_out, basis_in, *rest):
    bufs = rest[:CHUNKS]
    local_sem, near_sem, hist_send, hist_recv, send_sem, recv_sem = rest[CHUNKS:]
    f, c = lax.axis_index("freq"), lax.axis_index("clus")
    z, core = c // 2, c % 2
    levels = clusters // 2
    has_up, has_down = z + 1 < levels, z > 0
    up, down, partner = c + 2, c - 2, c + 1 - 2 * core
    chunk = near.shape[2]
    square = freqs == 4
    beside, across = f + 1 - 2 * (f % 2), (f + 2) % freqs
    peers = [beside, across] if square else [(f + i) % freqs for i in range(1, freqs)]

    loads = [
        pltpu.make_async_copy(own, hist.at[f], local_sem.at[0]),
        pltpu.make_async_copy(in_in, basis_in, local_sem.at[1]),
        pltpu.make_async_copy(out_in, basis_out, local_sem.at[2]),
        pltpu.make_async_copy(couple_in.at[0], couple, local_sem.at[3]),
    ]
    blocks = [
        pltpu.make_async_copy(near_in.at[0, :, pl.ds(w * chunk, chunk)], near.at[w], near_sem.at[w])
        for w in range(CHUNKS)
    ]

    barrier = pltpu.get_barrier_semaphore()
    for peer in peers:
        pl.semaphore_signal(barrier, inc=1, device_id=(peer, c), device_id_type=MESH)
    pl.semaphore_signal(barrier, inc=1, device_id=(f, partner), device_id_type=MESH)

    @pl.when(has_up)
    def _():
        pl.semaphore_signal(barrier, inc=1, device_id=(f, up), device_id_type=MESH)

    @pl.when(has_down)
    def _():
        pl.semaphore_signal(barrier, inc=1, device_id=(f, down), device_id_type=MESH)

    loads[0].start()
    pl.semaphore_wait(barrier, len(peers) + 1 + jnp.where(z + 1 < levels, 1, 0) + jnp.where(z > 0, 1, 0))

    exc = own.shape[0]
    halves = [pl.ds(0, exc // 2), pl.ds(exc // 2, exc // 2)]

    def give(peer, slot, part, source, number):
        return pltpu.make_async_remote_copy(
            src_ref=source, dst_ref=hist.at[slot, halves[part]],
            send_sem=hist_send.at[number], recv_sem=hist_recv.at[slot, part],
            device_id=(peer, c), device_id_type=MESH,
        )

    def arrived(slot, part):
        give(peers[0], slot, part, hist.at[slot, halves[part]], 0).wait_recv()

    sent = []
    for number, peer in enumerate(peers):
        for part in ((0, 1) if number % 2 == 0 else (1, 0)):
            sent.append(give(peer, f, part, own.at[halves[part]], 2 * number + part))
            sent[-1].start()
    for copy in loads[1:] + blocks:
        copy.start()
    fill_tables(c_re, c_im, f_re, f_im, table)
    if square:
        arrived(beside, 0)
        sent.append(give(across, beside, 0, hist.at[beside, halves[0]], 4))
        sent[-1].start()
        arrived(across, 1)
        sent.append(give(beside, across, 1, hist.at[across, halves[1]], 5))
        sent[-1].start()
        corner = (beside + 2) % freqs
        for slot, part in ((beside, 1), (across, 0), (corner, 0), (corner, 1)):
            arrived(slot, part)
    else:
        for peer in peers:
            for part in range(2):
                arrived(peer, part)
    for copy in sent:
        copy.wait_send()
    loads[0].wait()
    loads[1].wait()

    def pass_on(w, source, target, way):
        return pltpu.make_async_remote_copy(
            src_ref=bufs[w].at[source], dst_ref=bufs[w].at[source],
            send_sem=send_sem.at[w, source // 2, way], recv_sem=recv_sem.at[w, source],
            device_id=(f, target), device_id_type=MESH,
        )

    def when(flag, action):
        @pl.when(flag)
        def _():
            action()

    for w in range(CHUNKS):
        transform_chunk(w, hist, table, sums, bufs[w], c)
        compress_chunk(w, bufs[w], basis_in, c, chunk)
        when(has_up, lambda: pass_on(w, c, up, 0).start())
        when(has_down, lambda: pass_on(w, c, down, 1).start())
        pass_on(w, c, partner, 2).start()

    for copy in loads[2:]:
        copy.wait()
    picked = [mine[j] for j in range(near.shape[1])]
    for d in range(1, levels):
        for w in range(CHUNKS):
            below, above = c - 2 * d, c + 2 * d

            def from_below():
                pass_on(w, below, partner, 2).wait_recv()
                when(has_up, lambda: pass_on(w, below, up, 0).start())
                pass_on(w, below, partner, 2).start()

            def from_above():
                pass_on(w, above, partner, 2).wait_recv()
                when(has_down, lambda: pass_on(w, above, down, 1).start())
                pass_on(w, above, partner, 2).start()

            when(z >= d, from_below)
            when(z + d < levels, from_above)
    for w in range(CHUNKS):
        pass_on(w, partner, partner, 2).wait_recv()
        for d in range(1, levels):
            below, above = partner - 2 * d, partner + 2 * d
            when(z >= d, lambda: pass_on(w, below, partner, 2).wait_recv())
            when(z + d < levels, lambda: pass_on(w, above, partner, 2).wait_recv())
        blocks[w].wait()
        apply_chunk(w, picked, near, bufs[w], couple, basis_out, limit, out)

    for w in range(CHUNKS):
        when(has_up, lambda: pass_on(w, c, up, 0).wait_send())
        when(has_down, lambda: pass_on(w, c, down, 1).wait_send())
        pass_on(w, c, partner, 2).wait_send()
        for d in range(1, levels):
            below, above = c - 2 * d, c + 2 * d

            def below_sent():
                when(has_up, lambda: pass_on(w, below, up, 0).wait_send())
                pass_on(w, below, partner, 2).wait_send()

            def above_sent():
                when(has_down, lambda: pass_on(w, above, down, 1).wait_send())
                pass_on(w, above, partner, 2).wait_send()

            when(z >= d, below_sent)
            when(z + d < levels, above_sent)


def step_all(mine, factors, limit, turned, near_blocks, coupling, basis_out, basis_in, freqs, clusters):
    exc, length, panels = turned.shape
    waves, _, rank, _ = basis_in.shape
    slots = near_blocks.shape[1]
    chunk = waves // CHUNKS
    pack = LANES // rank
    rows = 2 * exc
    bf16 = jnp.bfloat16
    vmem, anywhere = pl.BlockSpec(memory_space=pltpu.VMEM), pl.BlockSpec(memory_space=pl.ANY)
    dma = pltpu.SemaphoreType.DMA
    return pl.pallas_call(
        functools.partial(kernel, freqs, clusters),
        out_shape=jax.ShapeDtypeStruct((waves, 2, exc, panels), bf16),
        in_specs=[pl.BlockSpec(memory_space=pltpu.SMEM)] + [vmem] * 6 + [anywhere] * 4,
        out_specs=vmem,
        scratch_shapes=[
            pltpu.VMEM((freqs, exc, length, panels), bf16),
            pltpu.VMEM((CHUNKS, 4 * chunk, freqs * length), bf16),
            pltpu.VMEM((chunk * rows, panels), jnp.float32),
            pltpu.VMEM((CHUNKS, slots, chunk, 2, panels, panels), bf16),
            pltpu.VMEM(coupling.shape[1:], bf16),
            pltpu.VMEM(basis_out.shape, bf16),
            pltpu.VMEM(basis_in.shape, bf16),
        ]
        + [pltpu.VMEM((clusters, chunk + chunk // pack, rows, panels), bf16)] * CHUNKS
        + [
            dma((4,)),
            dma((CHUNKS,)),
            dma((max(6, 2 * freqs),)),
            dma((freqs, 2)),
            dma((CHUNKS, clusters // 2, 3)),
            dma((CHUNKS, clusters)),
        ],
        compiler_params=pltpu.CompilerParams(
            collective_id=0, has_side_effects=True, vmem_limit_bytes=60 * 1024 * 1024
        ),
    )(mine, *factors, limit, turned, near_blocks, coupling, basis_out, basis_in)


def local(history, near_blocks, near_list, basis_out, basis_in, coupling, ranks):
    steps_dev, exc, panels = history.shape
    waves_dev, _, rank, _ = basis_in.shape
    clusters = lax.axis_size("clus")
    freqs = lax.axis_size("freq")
    total = steps_dev * freqs
    mine = lax.dynamic_index_in_dim(near_list, lax.axis_index("clus"), 0, keepdims=False)
    nearby = jnp.any(mine[:, None] == lax.iota(jnp.int32, clusters)[None, :], axis=0)
    far = jnp.where(nearby[None, :], 0, ranks[0])
    within = lax.iota(jnp.int32, rank)
    limit = jnp.where(within[None, None, :] < far[:, :, None], far[:, :, None], 0)
    limit = limit.reshape(waves_dev, clusters * rank)
    factors = wave_factors(lax.axis_index("freq") * waves_dev, waves_dev, total)
    turned = jnp.transpose(history, (1, 0, 2))
    return step_all(
        mine, factors, limit, turned, near_blocks, coupling, basis_out, basis_in, freqs, clusters
    )


def solution(mesh):
    placed = (
        P("freq", None, "clus"),
        P("clus", None, "freq", None, None, None),
        P(),
        P("freq", None, None, "clus"),
        P("freq", None, None, "clus"),
        P("clus", "freq", None, None, None),
        P("clus", "freq", None),
    )
    return jax.shard_map(
        local, mesh=mesh, in_specs=placed, out_specs=P("freq", None, None, "clus"), check_vma=False
    )
```

time: 168 us -> 103 us (0.61)
  waiting for transfers between devices: 107 us -> 0 us
  Pallas kernels: 39.6 us -> 93.8 us
  between operations: 13.2 us -> 0.05 us
    all_gather x3 -> x0, waiting for transfers between devices: 106 us -> none  [the longest x1 48.1 us: local(): dens = lax.all_gather(dens, 'clus', axis=0)]
    pallas_call x2 -> x1, Pallas kernels: 39.6 us -> 93.8 us  [step_all(): pl.pallas_call(functools.partial(kernel, freqs, clusters), out_shape=jax....]
    unnamed x7, local copies, waits for them, and re-layouts: 0.11 us -> 5.24 us
    all_gather x1 -> x0, local copies, waits for them, and re-layouts: 3.73 us -> none  [local(): hist = lax.all_gather(turned, 'freq', axis=0)]
  transfers between devices with their start and end apart: 3 -> 0, of which waited for: 3 -> 0; matrix products, arithmetic and copies ran while one was open for 2% -> 0% of each run, Pallas kernels for 0% -> 0%
where the time goes in v1:
time: 103 us; the launch traced here: 102 us
  Pallas kernels  93.8 us (91%)
  local copies, waits for them, and re-layouts  5.68 us (6%)
  other arithmetic  2.79 us (3%)
    pallas_call x1, Pallas kernels, step_all(): pl.pallas_call(functools.partial(kernel, freqs, clusters), out_shape=jax....  93.8 us
    unnamed x7, local copies, waits for them, and re-layouts  5.24 us

profile of v1, /device:TPU:0, one launch (start us, length us, event | category | flops | bytes accessed | tf_op | source)
XLA Modules:
  0.0 102.3 jit_solution(17020327710929069298)
XLA Ops:
  0.0 0.0 copy-start
  0.0 0.7 copy-done
  0.7 0.2 dynamic-slice_reduce_fusion.mine
  0.9 0.0 copy-start.1
  0.9 0.1 fusion.9
  1.0 0.1 lt.40
  1.1 0.8 copy.21
  2.0 0.1 copy.23
  2.1 0.7 compare_select_fusion.limit
  2.7 1.0 sine_multiply_fusion.1
  3.7 1.0 sine_multiply_fusion
  4.7 1.9 %copy.28 = bf16[256,8,128]{2,0,1:T(8,128)(2,1)} copy(bf16[256,8,128]{2,1,0:T(8,128)(2,1)} %param.7) | data formatting | bytes 1048576 | tf_op args[0]
  6.6 0.0 copy-done.1
  6.6 93.8 %shard_map.73 = bf16[128,2,8,128]{3,2,1,0:T(8,128)(2,1)} custom-call(s32[4]{0:T(128)} %copy-done.1, f32[128,8]{1,0:T(8,128)} %get-tuple-element.6.c_re, f32[128,8]{1,0:T(8,128)} %get-tuple-element.5.c_im, f32[128,128]{1,0:T(8,128)} %get-tuple-element.8.f_re, f32[128,128]{1,0:T(8,128)} %get-tuple-element.7.f_im, s32[128,256]{1,0:T(8,128)} %compare_select_fusion.limit, ...), custom_call_target="tpu_custom_call" | custom-call | tf_op jit(solution)/shard_map/pallas_call | solution.py:295
  100.4 1.9 %copy.30 = bf16[128,2,8,128]{3,2,1,0:T(8,128)(2,1)} copy(bf16[128,2,8,128]{3,2,1,0:T(8,128)(2,1)} %shard_map.73) | data formatting | bytes 1048576
  (8 shorter events, 0.1 us)
Async XLA Ops:
  0.0 0.7 copy-start
  0.9 5.8 %copy-start.1 = (s32[4]{0:T(128)}, s32[4]{0:T(128)S(1)}, u32[]{:S(2)}) copy-start(s32[4]{0:T(128)S(1)} %dynamic-slice_reduce_fusion.mine) | copy-start | bytes 52

commit v2 on v1

--- a/solution.py
+++ b/solution.py
@@ -68,7 +68,7 @@
     buf[me, pl.ds(0, chunk)] = sums[...].reshape(chunk, 2 * exc, LANES).astype(jnp.bfloat16)
 
 
-def compress_chunk(w, buf, basis_in, me, chunk):
+def compress_chunk(w, buf, coeffs, basis_in, me, chunk):
     rows, rank = buf.shape[2], basis_in.shape[2]
     half = rows // 2
     pack = LANES // rank
@@ -88,57 +88,76 @@
         by_re, by_im = pick(0), pick(1)
         real = by_re[:half] - by_im[half:]
         imag = by_re[half:] + by_im[:half]
-        buf[me, chunk + group] = jnp.concatenate([real, imag], 0).astype(jnp.bfloat16)
+        coeffs[me, w * (chunk // pack) + group] = jnp.concatenate([real, imag], 0).astype(jnp.bfloat16)
         return carry
 
     lax.fori_loop(0, chunk // pack, step, 0)
 
 
-def apply_chunk(w, picked, near, buf, couple, basis_out, limit, out):
-    slots, chunk = near.shape[1], near.shape[2]
-    panels, rank = near.shape[4], couple.shape[2]
-    sources, rows = buf.shape[0], buf.shape[2]
+def far_groups(first, count, coeffs, couple, basis_out, limit, far):
+    rank = couple.shape[2]
+    sources, rows = coeffs.shape[0], coeffs.shape[2]
     half = rows // 2
     pack = LANES // rank
+    unroll = min(2, count)
     position = lax.broadcasted_iota(jnp.int32, (rank, sources * rank), 0)
 
+    def step(pair, carry):
+        groups = [first + pair * unroll + u for u in range(unroll)]
+        waves = [(g * pack + i, i, u) for u, g in enumerate(groups) for i in range(pack)]
+        packed = [[coeffs[s, g].astype(jnp.float32) for s in range(sources)] for g in groups]
+        stacked = [
+            jnp.concatenate([p[:, i * rank : (i + 1) * rank] for p in packed[u]], axis=1).astype(jnp.bfloat16)
+            for _, i, u in waves
+        ]
+        mixes = []
+        for (wave, _, _), left in zip(waves, stacked):
+            keep = position < limit[pl.ds(wave, 1), :]
+            parts = [couple[wave, part] for part in range(2)]
+            mixes.append([dot(left, jnp.where(keep, v, jnp.zeros_like(v)), NT) for v in parts])
+        mixed = [
+            jnp.concatenate([r[:half] - m[half:], r[half:] + m[:half]], 0).astype(jnp.bfloat16)
+            for r, m in mixes
+        ]
+        spread = [[dot(m, basis_out[wave, part], NN) for part in range(2)] for (wave, _, _), m in zip(waves, mixed)]
+        for (wave, _, _), (r, m) in zip(waves, spread):
+            far[wave, pl.ds(0, half)] = r[:half] - m[half:]
+            far[wave, pl.ds(half, half)] = r[half:] + m[:half]
+        return carry
+
+    lax.fori_loop(0, count // unroll, step, 0)
+
+
+def near_chunk(w, picked, near, buf, far, out):
+    slots, chunk = near.shape[1], near.shape[2]
+    panels = near.shape[4]
+    half = buf.shape[2] // 2
+    unroll = 4
+
     def step(group, carry):
-        packed = [buf[s, chunk + group].astype(jnp.float32) for s in range(sources)]
-        for i in range(pack):
-            k = group * pack + i
-            wave = w * chunk + k
+        waves = [group * unroll + i for i in range(unroll)]
+        sums = []
+        for k in waves:
             left = jnp.concatenate([buf[s, k] for s in picked], axis=1)
             right = jnp.concatenate(
                 [near[w, j, k].reshape(2 * panels, panels) for j in range(slots)], axis=1
             )
-            both = dot(left, right, NT)
-            stacked = jnp.concatenate(
-                [p[:, i * rank : (i + 1) * rank] for p in packed], axis=1
-            ).astype(jnp.bfloat16)
-            keep = position < limit[pl.ds(wave, 1), :]
-
-            def mix(part):
-                value = couple[wave, part]
-                return dot(stacked, jnp.where(keep, value, jnp.zeros_like(value)), NT)
-
-            by_re, by_im = mix(0), mix(1)
-            mixed = jnp.concatenate(
-                [by_re[:half] - by_im[half:], by_re[half:] + by_im[:half]], 0
-            ).astype(jnp.bfloat16)
-            spread = jnp.concatenate([basis_out[wave, 0], basis_out[wave, 1]], axis=1)
-            both = both + dot(mixed, spread, NN)
+            sums.append(dot(left, right, NT))
+        for k, both in zip(waves, sums):
             by_re, by_im = both[:, :panels], both[:, panels:]
-            out[wave, 0] = (by_re[:half] - by_im[half:]).astype(out.dtype)
-            out[wave, 1] = (by_re[half:] + by_im[:half]).astype(out.dtype)
+            wave = w * chunk + k
+            out[wave, 0] = (by_re[:half] - by_im[half:] + far[wave, pl.ds(0, half)]).astype(out.dtype)
+            out[wave, 1] = (by_re[half:] + by_im[:half] + far[wave, pl.ds(half, half)]).astype(out.dtype)
         return carry
 
-    lax.fori_loop(0, chunk // pack, step, 0)
+    lax.fori_loop(0, chunk // unroll, step, 0)
 
 
 def kernel(freqs, clusters, mine, c_re, c_im, f_re, f_im, limit, own, near_in, couple_in, out_in, in_in,
            out, hist, table, sums, near, couple, basis_out, basis_in, *rest):
-    bufs = rest[:CHUNKS]
-    local_sem, near_sem, hist_send, hist_recv, send_sem, recv_sem = rest[CHUNKS:]
+    bufs = rest[: CHUNKS + 1]
+    coeffs = bufs[CHUNKS]
+    far, local_sem, near_sem, hist_send, hist_recv, send_sem, recv_sem = rest[CHUNKS + 1 :]
     f, c = lax.axis_index("freq"), lax.axis_index("clus")
     z, core = c // 2, c % 2
     levels = clusters // 2
@@ -228,42 +247,64 @@
         def _():
             action()
 
-    for w in range(CHUNKS):
-        transform_chunk(w, hist, table, sums, bufs[w], c)
-        compress_chunk(w, bufs[w], basis_in, c, chunk)
+    def send_own(w):
         when(has_up, lambda: pass_on(w, c, up, 0).start())
         when(has_down, lambda: pass_on(w, c, down, 1).start())
         pass_on(w, c, partner, 2).start()
 
+    early = CHUNKS // 2
+    for w in range(CHUNKS):
+        transform_chunk(w, hist, table, sums, bufs[w], c)
+        if w < early:
+            send_own(w)
+    for w in range(CHUNKS):
+        compress_chunk(w, bufs[w], coeffs, basis_in, c, chunk)
+    for w in [CHUNKS] + list(range(early, CHUNKS)):
+        send_own(w)
+
     for copy in loads[2:]:
         copy.wait()
     picked = [mine[j] for j in range(near.shape[1])]
-    for d in range(1, levels):
-        for w in range(CHUNKS):
-            below, above = c - 2 * d, c + 2 * d
-
-            def from_below():
-                pass_on(w, below, partner, 2).wait_recv()
-                when(has_up, lambda: pass_on(w, below, up, 0).start())
-                pass_on(w, below, partner, 2).start()
-
-            def from_above():
-                pass_on(w, above, partner, 2).wait_recv()
-                when(has_down, lambda: pass_on(w, above, down, 1).start())
-                pass_on(w, above, partner, 2).start()
-
-            when(z >= d, from_below)
-            when(z + d < levels, from_above)
-    for w in range(CHUNKS):
+    order = [CHUNKS] + list(range(CHUNKS))
+
+    def relay(w, d):
+        below, above = c - 2 * d, c + 2 * d
+
+        def from_below():
+            pass_on(w, below, partner, 2).wait_recv()
+            when(has_up, lambda: pass_on(w, below, up, 0).start())
+            pass_on(w, below, partner, 2).start()
+
+        def from_above():
+            pass_on(w, above, partner, 2).wait_recv()
+            when(has_down, lambda: pass_on(w, above, down, 1).start())
+            pass_on(w, above, partner, 2).start()
+
+        when(z >= d, from_below)
+        when(z + d < levels, from_above)
+
+    def complete(w):
         pass_on(w, partner, partner, 2).wait_recv()
         for d in range(1, levels):
             below, above = partner - 2 * d, partner + 2 * d
             when(z >= d, lambda: pass_on(w, below, partner, 2).wait_recv())
             when(z + d < levels, lambda: pass_on(w, above, partner, 2).wait_recv())
+
+    for d in range(1, levels - 1):
+        for w in order:
+            relay(w, d)
+    relay(CHUNKS, levels - 1)
+    complete(CHUNKS)
+    groups = coeffs.shape[1] // CHUNKS
+    for w in range(CHUNKS):
+        far_groups(w * groups, groups, coeffs, couple, basis_out, limit, far)
+        relay(w, levels - 1)
+    for w in range(CHUNKS):
+        complete(w)
         blocks[w].wait()
-        apply_chunk(w, picked, near, bufs[w], couple, basis_out, limit, out)
-
-    for w in range(CHUNKS):
+        near_chunk(w, picked, near, bufs[w], far, out)
+
+    for w in order:
         when(has_up, lambda: pass_on(w, c, up, 0).wait_send())
         when(has_down, lambda: pass_on(w, c, down, 1).wait_send())
         pass_on(w, c, partner, 2).wait_send()
@@ -306,14 +347,16 @@
             pltpu.VMEM(basis_out.shape, bf16),
             pltpu.VMEM(basis_in.shape, bf16),
         ]
-        + [pltpu.VMEM((clusters, chunk + chunk // pack, rows, panels), bf16)] * CHUNKS
+        + [pltpu.VMEM((clusters, chunk, rows, panels), bf16)] * CHUNKS
         + [
+            pltpu.VMEM((clusters, waves // pack, rows, LANES), bf16),
+            pltpu.VMEM((waves, rows, panels), jnp.float32),
             dma((4,)),
             dma((CHUNKS,)),
             dma((max(6, 2 * freqs),)),
             dma((freqs, 2)),
-            dma((CHUNKS, clusters // 2, 3)),
-            dma((CHUNKS, clusters)),
+            dma((CHUNKS + 1, clusters // 2, 3)),
+            dma((CHUNKS + 1, clusters)),
         ],
         compiler_params=pltpu.CompilerParams(
             collective_id=0, has_side_effects=True, vmem_limit_bytes=60 * 1024 * 1024

time: 103 us -> 91.4 us (0.89)
  Pallas kernels: 93.8 us -> 82.6 us
    pallas_call x1, Pallas kernels: 93.8 us -> 82.6 us  [step_all(): pl.pallas_call(functools.partial(kernel, freqs, clusters), out_shape=jax....]
where the time goes in v2:
time: 91.4 us; the launch traced here: 91.1 us
  Pallas kernels  82.6 us (90%)
  local copies, waits for them, and re-layouts  5.68 us (6%)
  other arithmetic  2.79 us (3%)
    pallas_call x1, Pallas kernels, step_all(): pl.pallas_call(functools.partial(kernel, freqs, clusters), out_shape=jax....  82.6 us
    unnamed x7, local copies, waits for them, and re-layouts  5.24 us
    mul x2, other arithmetic, factor(): return (weight[None, :] * jnp.cos(angle), -weight[None, :] * jnp.sin(angle))  2.01 us

profile of v2, /device:TPU:0, one launch (start us, length us, event | category | flops | bytes accessed | tf_op | source)
XLA Modules:
  0.0 91.1 jit_solution(9536380644114646292)
XLA Ops:
  0.0 0.0 copy-start
  0.0 0.7 copy-done
  0.7 0.2 dynamic-slice_reduce_fusion.mine
  0.9 0.0 copy-start.1
  0.9 0.1 fusion.9
  1.0 0.1 lt.40
  1.1 0.8 copy.21
  2.0 0.1 copy.23
  2.1 0.7 compare_select_fusion.limit
  2.7 1.0 %sine_multiply_fusion.1 = (f32[128,8]{1,0:T(8,128)}, f32[128,8]{1,0:T(8,128)}) fusion(f32[8]{0:T(128)S(1)} %get-tuple-element.10, s32[8]{0:T(128)S(1)} %iota_multiply_fusion, s32[128]{0:T(128)S(1)} %iota_add_fusion, f32[8]{0:T(128)S(1)} %get-tuple-element.9), kind=kLoop, calls=%fused_computation.21 | loop fusion | flops 16384 | bytes 8800 | tf_op jit(solution)/shard_map/mul | solution.py:26
  3.7 1.0 %sine_multiply_fusion = (f32[128,128]{1,0:T(8,128)}, f32[128,128]{1,0:T(8,128)}) fusion(f32[128]{0:T(128)S(1)} %get-tuple-element.12, s32[128]{0:T(128)S(1)} %iota_add_fusion, f32[128]{0:T(128)S(1)} %get-tuple-element.11), kind=kLoop, calls=%fused_computation.17 | loop fusion | flops 262144 | bytes 132608 | tf_op jit(solution)/shard_map/mul | solution.py:26
  4.7 1.9 %copy.28 = bf16[256,8,128]{2,0,1:T(8,128)(2,1)} copy(bf16[256,8,128]{2,1,0:T(8,128)(2,1)} %param.7) | data formatting | bytes 1048576 | tf_op args[0]
  6.6 0.0 copy-done.1
  6.6 82.6 %shard_map.73 = bf16[128,2,8,128]{3,2,1,0:T(8,128)(2,1)} custom-call(s32[4]{0:T(128)} %copy-done.1, f32[128,8]{1,0:T(8,128)} %get-tuple-element.6.c_re, f32[128,8]{1,0:T(8,128)} %get-tuple-element.5.c_im, f32[128,128]{1,0:T(8,128)} %get-tuple-element.8.f_re, f32[128,128]{1,0:T(8,128)} %get-tuple-element.7.f_im, s32[128,256]{1,0:T(8,128)} %compare_select_fusion.limit, ...), custom_call_target="tpu_custom_call" | custom-call | tf_op jit(solution)/shard_map/pallas_call | solution.py:336
  89.2 1.9 %copy.30 = bf16[128,2,8,128]{3,2,1,0:T(8,128)(2,1)} copy(bf16[128,2,8,128]{3,2,1,0:T(8,128)(2,1)} %shard_map.73) | data formatting | bytes 1048576
  (8 shorter events, 0.1 us)
Async XLA Ops:
  0.0 0.7 copy-start
  0.9 5.8 %copy-start.1 = (s32[4]{0:T(128)}, s32[4]{0:T(128)S(1)}, u32[]{:S(2)}) copy-start(s32[4]{0:T(128)S(1)} %dynamic-slice_reduce_fusion.mine) | copy-start | bytes 52

commit v3 on v2

--- a/solution.py
+++ b/solution.py
@@ -49,45 +49,55 @@
                     table[w, rows, a * LANES : (a + 1) * LANES] = held[w * chunk : (w + 1) * chunk]
 
 
-def transform_chunk(w, hist, table, sums, buf, me):
+def join(by_re, by_im, quarter):
+    real = [r[:quarter] - m[quarter:] for r, m in zip(by_re, by_im)]
+    imag = [r[quarter:] + m[:quarter] for r, m in zip(by_re, by_im)]
+    return jnp.concatenate(real, 0), jnp.concatenate(imag, 0)
+
+
+def transform_chunk(w, h, hist, table, sums, buf, me):
     blocks, exc, length = hist.shape[0], hist.shape[1], hist.shape[2]
     half = table.shape[1] // 2
     chunk = half // 2
-    for e in range(0, exc, 2):
+    quarter = exc // 2
+    for e in range(0, quarter, 2):
         value = None
         for f in range(blocks):
-            steps = jnp.concatenate([hist[f, e], hist[f, e + 1]], axis=1)
+            steps = jnp.concatenate([hist[f, h * quarter + e], hist[f, h * quarter + e + 1]], axis=1)
             term = dot(table[w, :, f * length : (f + 1) * length], steps, NN)
             value = term if value is None else value + term
         value = value[:half] + value[half:]
         for part in range(2):
             for side in range(2):
-                sums[pl.ds(part * exc + e + side, chunk, stride=2 * exc), :] = value[
+                sums[pl.ds(part * quarter + e + side, chunk, stride=exc), :] = value[
                     part * chunk : (part + 1) * chunk, side * LANES : (side + 1) * LANES
                 ]
-    buf[me, pl.ds(0, chunk)] = sums[...].reshape(chunk, 2 * exc, LANES).astype(jnp.bfloat16)
-
-
-def compress_chunk(w, buf, coeffs, basis_in, me, chunk):
-    rows, rank = buf.shape[2], basis_in.shape[2]
-    half = rows // 2
+    buf[me] = sums[...].reshape(chunk, exc, LANES).astype(jnp.bfloat16)
+
+
+def compress_chunk(w, pair, coeffs, basis_in, me):
+    chunk, exc, rank = pair[0].shape[1], pair[0].shape[2], basis_in.shape[2]
     pack = LANES // rank
-    lane = lax.broadcasted_iota(jnp.int32, (rows, LANES), 1) // rank
+    lane = lax.broadcasted_iota(jnp.int32, (exc, LANES), 1) // rank
 
     def step(group, carry):
-        left = buf[me, pl.ds(group * pack, pack)].reshape(pack * rows, LANES)
+        left = jnp.concatenate(
+            [buf[me, pl.ds(group * pack, pack)].reshape(pack * exc, LANES) for buf in pair], axis=0
+        )
 
         def pick(part):
             right = basis_in[pl.ds(w * chunk + group * pack, pack), part]
             full = dot(left, right.reshape(pack * rank, LANES), NT)
-            out = full[:rows]
-            for i in range(1, pack):
-                out = jnp.where(lane == i, full[i * rows : (i + 1) * rows], out)
-            return out
-
-        by_re, by_im = pick(0), pick(1)
-        real = by_re[:half] - by_im[half:]
-        imag = by_re[half:] + by_im[:half]
+            outs = []
+            for h in range(2):
+                rows = full[h * pack * exc : (h + 1) * pack * exc]
+                out = rows[:exc]
+                for i in range(1, pack):
+                    out = jnp.where(lane == i, rows[i * exc : (i + 1) * exc], out)
+                outs.append(out)
+            return outs
+
+        real, imag = join(pick(0), pick(1), exc // 2)
         coeffs[me, w * (chunk // pack) + group] = jnp.concatenate([real, imag], 0).astype(jnp.bfloat16)
         return carry
 
@@ -128,26 +138,30 @@
     lax.fori_loop(0, count // unroll, step, 0)
 
 
-def near_chunk(w, picked, near, buf, far, out):
+def near_chunk(w, picked, near, pair, far, out):
     slots, chunk = near.shape[1], near.shape[2]
     panels = near.shape[4]
-    half = buf.shape[2] // 2
+    exc = pair[0].shape[2]
     unroll = 4
 
     def step(group, carry):
         waves = [group * unroll + i for i in range(unroll)]
         sums = []
         for k in waves:
-            left = jnp.concatenate([buf[s, k] for s in picked], axis=1)
+            left = jnp.concatenate(
+                [jnp.concatenate([buf[s, k] for s in picked], axis=1) for buf in pair], axis=0
+            )
             right = jnp.concatenate(
                 [near[w, j, k].reshape(2 * panels, panels) for j in range(slots)], axis=1
             )
             sums.append(dot(left, right, NT))
         for k, both in zip(waves, sums):
-            by_re, by_im = both[:, :panels], both[:, panels:]
+            by_re = [both[:exc, :panels], both[exc:, :panels]]
+            by_im = [both[:exc, panels:], both[exc:, panels:]]
+            real, imag = join(by_re, by_im, exc // 2)
             wave = w * chunk + k
-            out[wave, 0] = (by_re[:half] - by_im[half:] + far[wave, pl.ds(0, half)]).astype(out.dtype)
-            out[wave, 1] = (by_re[half:] + by_im[:half] + far[wave, pl.ds(half, half)]).astype(out.dtype)
+            out[wave, 0] = (real + far[wave, pl.ds(0, exc)]).astype(out.dtype)
+            out[wave, 1] = (imag + far[wave, pl.ds(exc, exc)]).astype(out.dtype)
         return carry
 
     lax.fori_loop(0, chunk // unroll, step, 0)
@@ -155,9 +169,10 @@
 
 def kernel(freqs, clusters, mine, c_re, c_im, f_re, f_im, limit, own, near_in, couple_in, out_in, in_in,
            out, hist, table, sums, near, couple, basis_out, basis_in, *rest):
-    bufs = rest[: CHUNKS + 1]
-    coeffs = bufs[CHUNKS]
-    far, local_sem, near_sem, hist_send, hist_recv, send_sem, recv_sem = rest[CHUNKS + 1 :]
+    total = 2 * CHUNKS
+    bufs = rest[: total + 1]
+    coeffs = bufs[total]
+    far, local_sem, near_sem, hist_send, hist_recv, send_sem, recv_sem = rest[total + 1 :]
     f, c = lax.axis_index("freq"), lax.axis_index("clus")
     z, core = c // 2, c % 2
     levels = clusters // 2
@@ -195,45 +210,55 @@
     loads[0].start()
     pl.semaphore_wait(barrier, len(peers) + 1 + jnp.where(z + 1 < levels, 1, 0) + jnp.where(z > 0, 1, 0))
 
-    exc = own.shape[0]
-    halves = [pl.ds(0, exc // 2), pl.ds(exc // 2, exc // 2)]
+    quarter = own.shape[0] // 4
+    pieces = [pl.ds(q * quarter, quarter) for q in range(4)]
 
     def give(peer, slot, part, source, number):
         return pltpu.make_async_remote_copy(
-            src_ref=source, dst_ref=hist.at[slot, halves[part]],
-            send_sem=hist_send.at[number], recv_sem=hist_recv.at[slot, part],
+            src_ref=source.at[pieces[part]], dst_ref=hist.at[slot, pieces[part]],
+            send_sem=hist_send.at[number, part], recv_sem=hist_recv.at[slot, part],
             device_id=(peer, c), device_id_type=MESH,
         )
 
     def arrived(slot, part):
-        give(peers[0], slot, part, hist.at[slot, halves[part]], 0).wait_recv()
+        give(peers[0], slot, part, hist.at[slot], 0).wait_recv()
 
     sent = []
-    for number, peer in enumerate(peers):
-        for part in ((0, 1) if number % 2 == 0 else (1, 0)):
-            sent.append(give(peer, f, part, own.at[halves[part]], 2 * number + part))
-            sent[-1].start()
+
+    def send(*what):
+        sent.append(give(*what))
+        sent[-1].start()
+
+    def give_half(h):
+        for i in range(2):
+            for number, peer in enumerate(peers):
+                part = 2 * h + (i + number) % 2
+                send(peer, f, part, own, number)
+
+    def relay_half(h):
+        if square:
+            arrived(beside, 2 * h)
+            send(across, beside, 2 * h, hist.at[beside], len(peers))
+            arrived(across, 2 * h + 1)
+            send(beside, across, 2 * h + 1, hist.at[across], len(peers))
+
+    def finish_half(h):
+        if square:
+            corner = (beside + 2) % freqs
+            order = [(beside, 1), (across, 0), (corner, 0), (corner, 1)]
+        else:
+            order = [(peer, part) for peer in peers for part in range(2)]
+        for slot, part in order:
+            arrived(slot, 2 * h + part)
+
+    give_half(0)
     for copy in loads[1:] + blocks:
         copy.start()
     fill_tables(c_re, c_im, f_re, f_im, table)
-    if square:
-        arrived(beside, 0)
-        sent.append(give(across, beside, 0, hist.at[beside, halves[0]], 4))
-        sent[-1].start()
-        arrived(across, 1)
-        sent.append(give(beside, across, 1, hist.at[across, halves[1]], 5))
-        sent[-1].start()
-        corner = (beside + 2) % freqs
-        for slot, part in ((beside, 1), (across, 0), (corner, 0), (corner, 1)):
-            arrived(slot, part)
-    else:
-        for peer in peers:
-            for part in range(2):
-                arrived(peer, part)
-    for copy in sent:
-        copy.wait_send()
+    relay_half(0)
+    give_half(1)
+    finish_half(0)
     loads[0].wait()
-    loads[1].wait()
 
     def pass_on(w, source, target, way):
         return pltpu.make_async_remote_copy(
@@ -252,21 +277,6 @@
         when(has_down, lambda: pass_on(w, c, down, 1).start())
         pass_on(w, c, partner, 2).start()
 
-    early = CHUNKS // 2
-    for w in range(CHUNKS):
-        transform_chunk(w, hist, table, sums, bufs[w], c)
-        if w < early:
-            send_own(w)
-    for w in range(CHUNKS):
-        compress_chunk(w, bufs[w], coeffs, basis_in, c, chunk)
-    for w in [CHUNKS] + list(range(early, CHUNKS)):
-        send_own(w)
-
-    for copy in loads[2:]:
-        copy.wait()
-    picked = [mine[j] for j in range(near.shape[1])]
-    order = [CHUNKS] + list(range(CHUNKS))
-
     def relay(w, d):
         below, above = c - 2 * d, c + 2 * d
 
@@ -290,21 +300,53 @@
             when(z >= d, lambda: pass_on(w, below, partner, 2).wait_recv())
             when(z + d < levels, lambda: pass_on(w, above, partner, 2).wait_recv())
 
-    for d in range(1, levels - 1):
-        for w in order:
-            relay(w, d)
-    relay(CHUNKS, levels - 1)
-    complete(CHUNKS)
+    first, second = [2 * w for w in range(CHUNKS)], [2 * w + 1 for w in range(CHUNKS)]
+    for w in range(CHUNKS):
+        transform_chunk(w, 0, hist, table, sums, bufs[first[w]], c)
+        send_own(first[w])
+    relay_half(1)
+    if levels > 1:
+        for m in first:
+            relay(m, 1)
+    finish_half(1)
+    for w in range(CHUNKS):
+        transform_chunk(w, 1, hist, table, sums, bufs[second[w]], c)
+        send_own(second[w])
+    loads[1].wait()
+    for w in range(CHUNKS):
+        compress_chunk(w, (bufs[first[w]], bufs[second[w]]), coeffs, basis_in, c)
+    send_own(total)
+    for copy in loads[2:]:
+        copy.wait()
+    picked = [mine[j] for j in range(near.shape[1])]
+    last = levels - 1
+    for d in range(1, last):
+        if d > 1:
+            for m in first:
+                relay(m, d)
+            for m in [total] + second:
+                relay(m, d)
+        else:
+            for m in second[:2] + [total] + second[2:]:
+                relay(m, d)
+    if last > 1:
+        for m in first:
+            relay(m, last)
+    relay(total, last)
+    complete(total)
     groups = coeffs.shape[1] // CHUNKS
     for w in range(CHUNKS):
         far_groups(w * groups, groups, coeffs, couple, basis_out, limit, far)
-        relay(w, levels - 1)
+        relay(second[w], last)
     for w in range(CHUNKS):
-        complete(w)
+        complete(first[w])
+        complete(second[w])
         blocks[w].wait()
-        near_chunk(w, picked, near, bufs[w], far, out)
-
-    for w in order:
+        near_chunk(w, picked, near, (bufs[first[w]], bufs[second[w]]), far, out)
+
+    for copy in sent:
+        copy.wait_send()
+    for w in range(total + 1):
         when(has_up, lambda: pass_on(w, c, up, 0).wait_send())
         when(has_down, lambda: pass_on(w, c, down, 1).wait_send())
         pass_on(w, c, partner, 2).wait_send()
@@ -341,22 +383,22 @@
         scratch_shapes=[
             pltpu.VMEM((freqs, exc, length, panels), bf16),
             pltpu.VMEM((CHUNKS, 4 * chunk, freqs * length), bf16),
-            pltpu.VMEM((chunk * rows, panels), jnp.float32),
+            pltpu.VMEM((chunk * exc, panels), jnp.float32),
             pltpu.VMEM((CHUNKS, slots, chunk, 2, panels, panels), bf16),
             pltpu.VMEM(coupling.shape[1:], bf16),
             pltpu.VMEM(basis_out.shape, bf16),
             pltpu.VMEM(basis_in.shape, bf16),
         ]
-        + [pltpu.VMEM((clusters, chunk, rows, panels), bf16)] * CHUNKS
+        + [pltpu.VMEM((clusters, chunk, exc, panels), bf16)] * (2 * CHUNKS)
         + [
             pltpu.VMEM((clusters, waves // pack, rows, LANES), bf16),
             pltpu.VMEM((waves, rows, panels), jnp.float32),
             dma((4,)),
             dma((CHUNKS,)),
-            dma((max(6, 2 * freqs),)),
-            dma((freqs, 2)),
-            dma((CHUNKS + 1, clusters // 2, 3)),
-            dma((CHUNKS + 1, clusters)),
+            dma((freqs, 4)),
+            dma((freqs, 4)),
+            dma((2 * CHUNKS + 1, clusters // 2, 3)),
+            dma((2 * CHUNKS + 1, clusters)),
         ],
         compiler_params=pltpu.CompilerParams(
             collective_id=0, has_side_effects=True, vmem_limit_bytes=60 * 1024 * 1024

time: 91.4 us -> 87.3 us (0.955)
  Pallas kernels: 82.6 us -> 77.7 us
    pallas_call x1, Pallas kernels: 82.6 us -> 77.7 us  [step_all(): pl.pallas_call(functools.partial(kernel, freqs, clusters), out_shape=jax....]
where the time goes in v3:
time: 87.3 us; the launch traced here: 86.2 us
  Pallas kernels  77.7 us (89%)
  local copies, waits for them, and re-layouts  5.68 us (7%)
  other arithmetic  2.79 us (3%)
    pallas_call x1, Pallas kernels, step_all(): pl.pallas_call(functools.partial(kernel, freqs, clusters), out_shape=jax....  77.7 us
    unnamed x7, local copies, waits for them, and re-layouts  5.24 us
    mul x2, other arithmetic, factor(): return (weight[None, :] * jnp.cos(angle), -weight[None, :] * jnp.sin(angle))  2.01 us

profile of v3, /device:TPU:0, one launch (start us, length us, event | category | flops | bytes accessed | tf_op | source)
XLA Modules:
  0.0 86.2 jit_solution(2393973902948386552)
XLA Ops:
  0.0 0.0 copy-start
  0.0 0.7 copy-done
  0.7 0.2 dynamic-slice_reduce_fusion.mine
  0.9 0.0 copy-start.1
  0.9 0.1 fusion.9
  1.0 0.1 lt.40
  1.1 0.8 copy.21
  2.0 0.1 copy.23
  2.1 0.7 compare_select_fusion.limit
  2.7 1.0 %sine_multiply_fusion.1 = (f32[128,8]{1,0:T(8,128)}, f32[128,8]{1,0:T(8,128)}) fusion(f32[8]{0:T(128)S(1)} %get-tuple-element.10, s32[8]{0:T(128)S(1)} %iota_multiply_fusion, s32[128]{0:T(128)S(1)} %iota_add_fusion, f32[8]{0:T(128)S(1)} %get-tuple-element.9), kind=kLoop, calls=%fused_computation.21 | loop fusion | flops 16384 | bytes 8800 | tf_op jit(solution)/shard_map/mul | solution.py:26
  3.7 1.0 %sine_multiply_fusion = (f32[128,128]{1,0:T(8,128)}, f32[128,128]{1,0:T(8,128)}) fusion(f32[128]{0:T(128)S(1)} %get-tuple-element.12, s32[128]{0:T(128)S(1)} %iota_add_fusion, f32[128]{0:T(128)S(1)} %get-tuple-element.11), kind=kLoop, calls=%fused_computation.17 | loop fusion | flops 262144 | bytes 132608 | tf_op jit(solution)/shard_map/mul | solution.py:26
  4.7 1.9 %copy.28 = bf16[256,8,128]{2,0,1:T(8,128)(2,1)} copy(bf16[256,8,128]{2,1,0:T(8,128)(2,1)} %param.7) | data formatting | bytes 1048576 | tf_op args[0]
  6.6 0.0 copy-done.1
  6.6 77.7 %shard_map.73 = bf16[128,2,8,128]{3,2,1,0:T(8,128)(2,1)} custom-call(s32[4]{0:T(128)} %copy-done.1, f32[128,8]{1,0:T(8,128)} %get-tuple-element.6.c_re, f32[128,8]{1,0:T(8,128)} %get-tuple-element.5.c_im, f32[128,128]{1,0:T(8,128)} %get-tuple-element.8.f_re, f32[128,128]{1,0:T(8,128)} %get-tuple-element.7.f_im, s32[128,256]{1,0:T(8,128)} %compare_select_fusion.limit, ...), custom_call_target="tpu_custom_call" | custom-call | tf_op jit(solution)/shard_map/pallas_call | solution.py:378
  84.3 1.9 %copy.30 = bf16[128,2,8,128]{3,2,1,0:T(8,128)(2,1)} copy(bf16[128,2,8,128]{3,2,1,0:T(8,128)(2,1)} %shard_map.73) | data formatting | bytes 1048576
  (8 shorter events, 0.1 us)
Async XLA Ops:
  0.0 0.7 copy-start
  0.9 5.8 %copy-start.1 = (s32[4]{0:T(128)}, s32[4]{0:T(128)S(1)}, u32[]{:S(2)}) copy-start(s32[4]{0:T(128)S(1)} %dynamic-slice_reduce_fusion.mine) | copy-start | bytes 52
